TPU v7x, 32 devices: a whole 2x2x4 slice. The times are simulated.
32 devices in a mesh: freq: 4 (over z), chan: 8 (over y, x, core).
Axes of the slice: x: 2, y: 2, z: 4, core: 2. Of those that a mesh axis runs over, the one named last changes fastest.
Arguments:
- raw_strain: bfloat16 [8, 32, 150000], P('chan', 'freq'), may hold values from -6 to 6
- fir_taps: bfloat16 [20], replicated, may hold values from -1.25 to 1.25
- band_bins: int32 [240], replicated, may hold values from 60 to 359, as said below
- live_mask: int32 [8, 32], P('chan', 'freq'), may hold values 0 or 1
Outputs:
- cross_spectra: float32 [240, 2, 256, 256], P('freq', None, 'chan')
Inputs may be any that keep to these rules, and one draw needn't show every extreme that they name: `band_bins`: strictly increasing; the first is 60 and the last is 359.
All inputs are finite; a program needn't handle non-finite values. No bound on the sum of `live_mask` on one device may be relied on, other than what follows from the above.
Results may differ from a plain program's by a relative error of at most 0.0067.
Values may be sent and summed in bfloat16 or wider, within the bound.
No kernel may reach another device: no remote copies, remote signals or barrier semaphores. Data moves between devices by JAX's collectives and lax.ppermute only.
A program may use at most 64 MiB of HBM per device.

v0:
```python
import math
import jax
import jax.numpy as jnp
from jax import lax
from jax.sharding import PartitionSpec as P

WIN = 10
DECIM = 10
NT = 1500


def make_table(band_bins, length):
    times = jnp.arange(length, dtype=jnp.int32)[:, None]
    phase = times * band_bins[None, :] % length
    angle = phase.astype(jnp.float32) * jnp.float32(2.0 * math.pi / length)
    return jnp.concatenate([jnp.cos(angle), -jnp.sin(angle)], axis=1).astype(jnp.bfloat16)


def correlate(rows_spec, cols_spec, windows):
    bins = rows_spec.shape[0]
    height = rows_spec.shape[3]
    width = cols_spec.shape[3]
    real_left = rows_spec.reshape(bins, 2 * windows, height)
    imag_left = jnp.concatenate([rows_spec[:, 1], -rows_spec[:, 0]], axis=1)
    left_both = jnp.stack([real_left, imag_left], axis=1)
    right_side = cols_spec.reshape(bins, 2 * windows, width)
    prod = jnp.einsum("fski,fkj->fsij", left_both, right_side, preferred_element_type=jnp.float32)
    return prod / windows


def decimate(raw_strain, fir_taps, rows, windows, length, factor):
    outputs = length // 10
    span = outputs * factor
    blocks = raw_strain.reshape(rows * windows * 10, span)
    taps_float = fir_taps.astype(jnp.float32)
    tap_count = fir_taps.shape[0]
    sample_idx = jnp.arange(span, dtype=jnp.int32)[:, None]
    out_idx = jnp.arange(outputs, dtype=jnp.int32)[None, :]
    tap_idx = factor * out_idx + factor - 1 - sample_idx
    valid = (tap_idx >= 0) & (tap_idx < tap_count)
    band = jnp.where(valid, taps_float[jnp.clip(tap_idx, 0, tap_count - 1)], 0.0).astype(
        jnp.bfloat16
    )
    current = jnp.dot(blocks, band, preferred_element_type=jnp.float32)
    tail = blocks[:, span - factor :]
    tail_taps = taps_float[2 * factor - 1 - jnp.arange(factor, dtype=jnp.int32)].astype(
        jnp.bfloat16
    )
    carried = jnp.dot(tail, tail_taps[:, None], preferred_element_type=jnp.float32)
    carried = carried.reshape(rows * windows, 10)
    carried = jnp.pad(carried, ((0, 0), (1, 0)))[:, :10]
    current = current.reshape(rows * windows, 10, outputs)
    current = current.at[:, :, 0].add(carried)
    return current.reshape(rows, windows, length).astype(jnp.bfloat16)


def shards(raw_strain, fir_taps, band_bins, live_mask):
    rows = raw_strain.shape[1]
    windows = WIN
    length = NT
    factor = DECIM
    bins = band_bins.shape[0]
    table = make_table(band_bins, length)
    decimated = decimate(raw_strain, fir_taps, rows, windows, length, factor)
    spectrum = jnp.dot(
        decimated.reshape(rows * windows, length), table, preferred_element_type=jnp.float32
    )
    spectrum = spectrum.reshape(rows, windows, 2, bins)
    power = jnp.sum(spectrum * spectrum, axis=(2, 3)) / bins
    scale = lax.rsqrt(power + 1e-06) * live_mask[0].astype(jnp.float32)[:, None]
    whitened = (spectrum * scale[:, :, None, None]).astype(jnp.bfloat16)
    ordered = jnp.transpose(whitened, (3, 2, 1, 0))
    own = lax.all_to_all(ordered, "freq", split_axis=0, concat_axis=3, tiled=True)
    return correlate(own, lax.all_gather(own, "chan", axis=3, tiled=True), windows)


def solution(mesh):
    in_specs = (P("chan", "freq", None), P(), P(), P("chan", "freq"))
    out_specs = P("freq", None, "chan", None)
    return jax.shard_map(shards, mesh=mesh, in_specs=in_specs, out_specs=out_specs, check_vma=False)
```

profile of v0, /device:TPU:0, one launch (start us, length us, event | category | flops | bytes accessed | tf_op | source)
XLA Modules:
  0.0 82.6 jit_solution(9209558224427891211)
XLA Ops:
  0.0 2.1 %fusion.129 = (bf16[1]{0:T(256)(128)(2,1)}, bf16[1]{0:T(256)(128)(2,1)}, bf16[1]{0:T(256)(128)(2,1)}, bf16[1]{0:T(256)(128)(2,1)}, bf16[1]{0:T(256)(128)(2,1)}, ...) fusion(bf16[20]{0:T(256)(128)(2,1)} %param.7), kind=kLoop, calls=%fused_computation.157 | loop fusion | bytes 76 | tf_op jit(solution)/shard_map/gather | solution.py:41
  2.1 1.2 %slice.57 = bf16[1]{0:T(256)(128)(2,1)} slice(bf16[20]{0:T(256)(128)(2,1)} %param.7), slice={[17:18]} | slice | bytes 4 | tf_op jit(solution)/shard_map/gather | solution.py:41
  3.3 4.8 %reshape.254 = bf16[1200000]{0:T(1024)(128)(2,1)S(1)} reshape(bf16[1,8,150000]{2,1,0:T(8,128)(2,1)} %param.6) | data formatting | bytes 4800000
  8.1 5.1 %reshape.153 = bf16[800,1500]{1,0:T(8,128)(2,1)} reshape(bf16[1200000]{0:T(1024)(128)(2,1)S(1)} %reshape.254) | data formatting | bytes 4800000 | tf_op jit(solution)/shard_map/reshape | solution.py:34
  13.3 1.0 %slice.63 = bf16[800,10]{1,0:T(8,128)(2,1)S(1)} slice(bf16[800,1500]{1,0:T(8,128)(2,1)} %reshape.153), slice={[0:800], [1490:1500]} | slice | bytes 32000 | tf_op jit(solution)/shard_map/slice | solution.py:45
  14.3 17.4 %convolution_bitcast_fusion = f32[800,150]{0,1:T(8,128)S(1)} fusion(bf16[800,1500]{1,0:T(8,128)(2,1)} %reshape.153, bf16[]{:T(256)} %bitcast.27, bf16[]{:T(256)} %bitcast.28, bf16[]{:T(256)} %bitcast.29, bf16[]{:T(256)} %bitcast.30, bf16[]{:T(256)} %bitcast.31, bf16[]{:T(256)} %bitcast.33, bf16[]{:T(256)} %bitcast.32, bf16[]{:T(256)} %bitcast.2, ...), kind=kOutput, calls=%fused_computation.64 | convolution fusion | flops 370800000 | bytes 2880640 | tf_op jit(solution)/shard_map/dot_general | solution.py:44
  31.7 0.3 copy.30
  32.0 0.0 copy-start
  32.0 0.1 reshape.154
  32.1 0.1 copy.52
  32.3 0.2 dot_general.24
  32.5 0.1 copy-done
  32.6 0.7 gather_fusion
  33.3 0.1 multiply_reduce_fusion
  33.4 0.1 copy.44
  33.5 0.4 copy.32
  33.9 0.1 slice_add_fusion
  34.0 5.3 %scatter-add.4 = f32[80,10,150]{2,1,0:T(8,128)S(1)} dynamic-update-slice(f32[80,10,150]{2,1,0:T(8,128)S(1)} %reshape.154, f32[80,10,1]{2,1,0:T(8,128)S(1)} %slice_add_fusion, s32[]{:T(128)} %constant.58.clone.1, s32[]{:T(128)} %constant.58.clone.1, s32[]{:T(128)} %constant.58.clone.1) | dynamic-update-slice | bytes 6404 | tf_op jit(solution)/shard_map/scatter-add | solution.py:53
  39.3 0.0 copy-start.1
  39.3 0.1 convert_element_type.42
  39.4 0.0 copy-start.2
  39.4 0.7 reshape.250
  40.1 0.0 copy-done.1
  40.1 6.6 %cosine_convert_fusion = (bf16[1500,240]{0,1:T(8,128)(2,1)S(1)}, bf16[1500,240]{0,1:T(8,128)(2,1)S(1)}) fusion(s32[240]{0:T(256)S(1)} %copy-done.1), kind=kLoop, calls=%fused_computation.59 | loop fusion | flops 4320000 | bytes 1440960 | tf_op jit(solution)/shard_map/convert
  46.7 0.0 copy-done.2
  46.7 0.1 pad_maximum_fusion
  46.8 0.7 multiply_reduce_fusion.1
  47.5 0.1 multiply_bitcast_fusion
  47.6 0.1 fusion.103
  47.7 1.3 %copy.33 = bf16[240,2,10,8]{2,1,3,0:T(2,128)(2,1)S(1)} copy(bf16[240,2,10,8]{0,2,1,3:T(8,128)(2,1)S(1)} %fusion.103) | data formatting | bytes 153600 | tf_op jit(solution)/shard_map/convert_element_type | solution.py:71
  49.0 1.6 %reshape.256 = bf16[4,2,4800]{2,1,0:T(2,128)(2,1)S(1)} reshape(bf16[240,8,2,10]{3,2,1,0:T(2,128)(2,1)S(1)} %bitcast.166) | data formatting | bytes 153600
  50.5 11.9 %all_to_all.18 = bf16[4,2,4800]{2,1,0:T(2,128)(2,1)S(1)} all-to-all(bf16[4,2,4800]{2,1,0:T(2,128)(2,1)S(1)} %reshape.256), channel_id=1, replica_groups=mesh['freq'=4,'chan'=8] {'freq'}, dimensions={0} | all-to-all | bytes 153600 | tf_op jit(solution)/shard_map/all_to_all | solution.py:73
  62.4 2.3 %reshape.257 = bf16[240,8,2,10]{3,2,1,0:T(2,128)(2,1)S(1)} reshape(bf16[4,2,4800]{2,1,0:T(2,128)(2,1)S(1)} %all_to_all.18) | data formatting | bytes 153600
  64.8 1.3 %copy.47 = bf16[4,60,2,10,8]{1,0,4,3,2:T(4,128)(2,1)S(1)} copy(bf16[4,60,2,10,8]{3,2,4,1,0:T(2,128)(2,1)S(1)} %bitcast.167) | data formatting | bytes 153600 | tf_op jit(solution)/shard_map/all_to_all | solution.py:73
  66.1 12.1 %all_gather.3 = bf16[60,2,10,256]{0,3,2,1:T(8,128)(2,1)S(1)} all-gather(bf16[60,2,10,32]{0,3,2,1:T(8,128)(2,1)S(1)} %bitcast.168), channel_id=1, replica_groups=mesh['freq'=4,'chan'=8] {'chan'}, dimensions={3}, use_global_device_ids=true | all-gather | bytes 691200 | tf_op jit(solution)/shard_map/all_gather | solution.py:74
  78.3 0.9 %copy.46 = bf16[60,20,256,1]{2,1,3,0:T(8,128)(2,1)S(1)} copy(bf16[60,20,256,1]{0,2,1,3:T(8,128)(2,1)S(1)} %bitcast.165) | data formatting | bytes 1228800 | tf_op jit(solution)/shard_map/reshape | solution.py:26
  79.2 0.1 pad_maximum_fusion.1
  79.3 0.6 copy.38
  79.9 2.7 %convolution_multiply_fusion = f32[60,2,32,256]{3,2,1,0:T(8,128)} fusion(bf16[60,2,20,32]{3,2,1,0:T(8,128)(2,1)S(1)} %copy.38, bf16[60,20,256,1]{2,1,3,0:T(8,128)(2,1)S(1)} %copy.46), kind=kOutput, calls=%fused_computation.3 | convolution fusion | flops 40304640 | bytes 4700160 | tf_op jit(solution)/shard_map/fski,fkj->fsij/dot_general | solution.py:27
  (9 shorter events, 0.1 us)
Async XLA Ops:
  32.0 0.7 copy-start
  39.3 0.8 copy-start.1
  39.4 7.3 %copy-start.2 = (s32[1,8]{1,0:T(1,128)S(1)}, s32[1,8]{1,0:T(1,128)}, u32[]{:S(2)}) copy-start(s32[1,8]{1,0:T(1,128)} %param.9) | copy-start | bytes 100
where the time goes:
time: 83.1 us; the launch traced here: 82.6 us
  local copies, waits for them, and re-layouts  30.3 us (36%)
  blocking collectives  24 us (29%)
  matrix products  20.8 us (25%)
  other arithmetic  7.29 us (9%)
    dot_general x1, matrix products, decimate(): current = jnp.dot(blocks, band, preferred_element_type=jnp.float32)  17.4 us
    all_gather x1, blocking collectives, shards(): lax.all_gather(own, 'chan', axis=3, tiled=True)  12.1 us
    all_to_all x1, blocking collectives, shards(): lax.all_to_all(ordered, 'freq', split_axis=0, concat_axis=3, tiled=True)  11.9 us
    unnamed x10, local copies, waits for them, and re-layouts  8.94 us
    another operation x1, other arithmetic  6.55 us
    scatter-add x1, local copies, waits for them, and re-layouts, decimate(): current = current.at[:, :, 0].add(carried)  5.28 us
    reshape x1, local copies, waits for them, and re-layouts, decimate(): blocks = raw_strain.reshape(rows * windows * 10, span)  5.14 us
    gather x2, local copies, waits for them, and re-layouts, decimate(): taps_float[jnp.clip(tap_idx, 0, tap_count - 1)]  3.32 us

commit v1 on v0

--- a/solution.py
+++ b/solution.py
@@ -70,7 +70,10 @@
     scale = lax.rsqrt(power + 1e-06) * live_mask[0].astype(jnp.float32)[:, None]
     whitened = (spectrum * scale[:, :, None, None]).astype(jnp.bfloat16)
     ordered = jnp.transpose(whitened, (3, 2, 1, 0))
-    own = lax.all_to_all(ordered, "freq", split_axis=0, concat_axis=3, tiled=True)
+    peers = lax.axis_size("freq")
+    shards_2 = jnp.stack(jnp.split(ordered, peers, axis=0), axis=0)
+    shards_2 = lax.all_to_all(shards_2, "freq", split_axis=0, concat_axis=0)
+    own = jnp.concatenate(shards_2, axis=3)
     return correlate(own, lax.all_gather(own, "chan", axis=3, tiled=True), windows)
 
 

time: 83.1 us -> 78.1 us (0.940)
  local copies, waits for them, and re-layouts: 30.3 us -> 25 us
    unnamed x10, local copies, waits for them, and re-layouts: 8.94 us -> 5.61 us
    all_to_all x2 -> x1, local copies, waits for them, and re-layouts: 1.36 us -> 0.04 us  [shards(): shards_2 = lax.all_to_all(shards_2, 'freq', split_axis=0, concat_axis=0)]
    convert_element_type x1 -> x0, local copies, waits for them, and re-layouts: 1.26 us -> none  [shards(): whitened = (spectrum * scale[:, :, None, None]).astype(jnp.bfloat16)]
    all_gather x0 -> x1, local copies, waits for them, and re-layouts: none -> 1.15 us  [shards(): lax.all_gather(own, 'chan', axis=3, tiled=True)]
    another operation x1 -> x2, other arithmetic: 6.55 us -> 6.63 us
where the time goes in v1:
time: 78.1 us; the launch traced here: 77.6 us
  local copies, waits for them, and re-layouts  25 us (32%)
  blocking collectives  24 us (31%)
  matrix products  20.9 us (27%)
  other arithmetic  7.37 us (9%)
    dot_general x1, matrix products, decimate(): current = jnp.dot(blocks, band, preferred_element_type=jnp.float32)  17.4 us
    all_gather x1, blocking collectives, shards(): lax.all_gather(own, 'chan', axis=3, tiled=True)  12.1 us
    all_to_all x1, blocking collectives, shards(): shards_2 = lax.all_to_all(shards_2, 'freq', split_axis=0, concat_axis=0)  11.9 us
    another operation x1, other arithmetic  6.55 us
    unnamed x10, local copies, waits for them, and re-layouts  5.61 us
    scatter-add x1, local copies, waits for them, and re-layouts, decimate(): current = current.at[:, :, 0].add(carried)  5.28 us
    reshape x1, local copies, waits for them, and re-layouts, decimate(): blocks = raw_strain.reshape(rows * windows * 10, span)  5.14 us
    gather x2, local copies, waits for them, and re-layouts, decimate(): taps_float[jnp.clip(tap_idx, 0, tap_count - 1)]  3.33 us

profile of v1, /device:TPU:0, one launch (start us, length us, event | category | flops | bytes accessed | tf_op | source)
XLA Modules:
  0.0 77.6 jit_solution(2513810363816606618)
XLA Ops:
  0.0 2.1 %fusion.130 = (bf16[1]{0:T(256)(128)(2,1)}, bf16[1]{0:T(256)(128)(2,1)}, bf16[1]{0:T(256)(128)(2,1)}, bf16[1]{0:T(256)(128)(2,1)}, bf16[1]{0:T(256)(128)(2,1)}, ...) fusion(bf16[20]{0:T(256)(128)(2,1)} %param.7), kind=kLoop, calls=%fused_computation.163 | loop fusion | bytes 76 | tf_op jit(solution)/shard_map/gather | solution.py:41
  2.1 1.3 %slice.57 = bf16[1]{0:T(256)(128)(2,1)} slice(bf16[20]{0:T(256)(128)(2,1)} %param.7), slice={[17:18]} | slice | bytes 4 | tf_op jit(solution)/shard_map/gather | solution.py:41
  3.3 4.8 %reshape.261 = bf16[1200000]{0:T(1024)(128)(2,1)S(1)} reshape(bf16[1,8,150000]{2,1,0:T(8,128)(2,1)} %param.6) | data formatting | bytes 4800000
  8.1 5.1 %reshape.158 = bf16[800,1500]{1,0:T(8,128)(2,1)} reshape(bf16[1200000]{0:T(1024)(128)(2,1)S(1)} %reshape.261) | data formatting | bytes 4800000 | tf_op jit(solution)/shard_map/reshape | solution.py:34
  13.3 1.0 %slice.63 = bf16[800,10]{1,0:T(8,128)(2,1)S(1)} slice(bf16[800,1500]{1,0:T(8,128)(2,1)} %reshape.158), slice={[0:800], [1490:1500]} | slice | bytes 32000 | tf_op jit(solution)/shard_map/slice | solution.py:45
  14.3 17.4 %convolution_bitcast_fusion = f32[800,150]{0,1:T(8,128)S(1)} fusion(bf16[800,1500]{1,0:T(8,128)(2,1)} %reshape.158, bf16[]{:T(256)} %bitcast.27, bf16[]{:T(256)} %bitcast.28, bf16[]{:T(256)} %bitcast.29, bf16[]{:T(256)} %bitcast.30, bf16[]{:T(256)} %bitcast.31, bf16[]{:T(256)} %bitcast.33, bf16[]{:T(256)} %bitcast.32, bf16[]{:T(256)} %bitcast.2, ...), kind=kOutput, calls=%fused_computation.64 | convolution fusion | flops 370800000 | bytes 2880640 | tf_op jit(solution)/shard_map/dot_general | solution.py:44
  31.7 0.3 copy.27
  32.0 0.0 copy-start
  32.0 0.1 reshape.159
  32.1 0.1 copy.45
  32.3 0.2 dot_general.24
  32.5 0.1 copy-done
  32.6 0.7 gather_fusion
  33.3 0.1 multiply_reduce_fusion
  33.4 0.1 copy.40
  33.5 0.4 copy.29
  33.9 0.1 slice_add_fusion
  34.0 5.3 %scatter-add.4 = f32[80,10,150]{2,1,0:T(8,128)S(1)} dynamic-update-slice(f32[80,10,150]{2,1,0:T(8,128)S(1)} %reshape.159, f32[80,10,1]{2,1,0:T(8,128)S(1)} %slice_add_fusion, s32[]{:T(128)} %constant.58.clone.1, s32[]{:T(128)} %constant.58.clone.1, s32[]{:T(128)} %constant.58.clone.1) | dynamic-update-slice | bytes 6404 | tf_op jit(solution)/shard_map/scatter-add | solution.py:53
  39.3 0.0 copy-start.1
  39.3 0.1 convert_element_type.42
  39.4 0.0 copy-start.2
  39.4 0.7 reshape.257
  40.1 0.0 copy-done.1
  40.1 6.6 %cosine_convert_fusion = (bf16[1500,240]{0,1:T(8,128)(2,1)S(1)}, bf16[1500,240]{0,1:T(8,128)(2,1)S(1)}) fusion(s32[240]{0:T(256)S(1)} %copy-done.1), kind=kLoop, calls=%fused_computation.59 | loop fusion | flops 4320000 | bytes 1440960 | tf_op jit(solution)/shard_map/convert
  46.7 0.0 copy-done.2
  46.7 0.1 pad_maximum_fusion
  46.8 0.7 multiply_reduce_fusion.1
  47.5 0.1 multiply_bitcast_fusion
  47.6 0.1 fusion.104
  47.7 0.1 slice_bitcast_fusion.4
  47.8 0.1 pad_maximum_fusion.2
  47.9 0.1 copy.51
  48.0 0.3 reshape.263
  48.2 11.9 %all_to_all.5 = bf16[4,2,4800]{2,1,0:T(2,128)(2,1)S(1)} all-to-all(bf16[4,2,4800]{2,1,0:T(2,128)(2,1)S(1)} %reshape.263), channel_id=1, replica_groups=mesh['freq'=4,'chan'=8] {'freq'}, dimensions={0} | all-to-all | bytes 153600 | tf_op jit(solution)/shard_map/all_to_all | solution.py:75
  60.2 0.3 reshape.264
  60.5 0.2 copy.32
  60.7 12.1 %all_gather.3 = bf16[60,2,10,256]{0,1,2,3:T(2,128)(2,1)S(1)} all-gather(bf16[60,2,10,32]{0,1,2,3:T(2,128)(2,1)S(1)} %copy.32), channel_id=1, replica_groups=mesh['freq'=4,'chan'=8] {'chan'}, dimensions={3}, use_global_device_ids=true | all-gather | bytes 691200 | tf_op jit(solution)/shard_map/all_gather | solution.py:77
  72.8 1.1 %copy.33 = bf16[60,2,10,256]{3,0,2,1:T(8,128)(2,1)S(1)} copy(bf16[60,2,10,256]{0,1,2,3:T(2,128)(2,1)S(1)} %all_gather.3) | data formatting | bytes 1228800 | tf_op jit(solution)/shard_map/all_gather | solution.py:77
  74.0 0.1 pad_maximum_fusion.1
  74.1 0.6 copy.34
  74.7 2.9 %convolution_multiply_fusion = f32[60,2,32,256]{3,2,1,0:T(8,128)} fusion(bf16[60,2,20,32]{3,2,1,0:T(8,128)(2,1)S(1)} %copy.34, bf16[60,20,256,1]{2,0,1,3:T(8,128)(2,1)S(1)} %bitcast.177), kind=kOutput, calls=%fused_computation.3 | convolution fusion | flops 40304640 | bytes 4700160 | tf_op jit(solution)/shard_map/fski,fkj->fsij/dot_general | solution.py:27
  (9 shorter events, 0.1 us)
Async XLA Ops:
  32.0 0.7 copy-start
  39.3 0.8 %copy-start.1 = (s32[240]{0:T(256)S(1)}, s32[240]{0:T(256)}, u32[]{:S(2)}) copy-start(s32[240]{0:T(256)} %param.8) | copy-start | bytes 2884
  39.4 7.3 %copy-start.2 = (s32[1,8]{1,0:T(1,128)S(1)}, s32[1,8]{1,0:T(1,128)}, u32[]{:S(2)}) copy-start(s32[1,8]{1,0:T(1,128)} %param.9) | copy-start | bytes 100
